TPU v7x, 128 devices: a whole 4x4x4 slice. The times are simulated.
128 devices in a mesh: row: 8 (over x, core), col: 16 (over z, y).
Axes of the slice: x: 4, y: 4, z: 4, core: 2. Of those that a mesh axis runs over, the one named last changes fastest.
Arguments:
- model_init: float32 [2, 2, 16, 16384], P(None, None, None, 'col'), may hold values from -2 to 2
- observed: float32 [2, 2, 16, 32768], P(None, None, None, ('row', 'col')), may hold values from -6 to 6
- left_bases: bfloat16 [128, 64, 2, 96, 2, 256], P(('row', 'col')), may hold values from -0.078125 to 0.078125
- right_bases: bfloat16 [128, 64, 2, 96, 2, 256], P('row', 'col'), may hold values from -0.078125 to 0.078125
- tile_ranks: int32 [128, 64, 2], P('row', 'col'), may hold values from 8 to 96
- gate_start: int32 [16, 32768], P(None, ('row', 'col')), may hold values from 0 to 31
- gate_stop: int32 [16, 32768], P(None, ('row', 'col')), may hold values from 32 to 64
Outputs:
- model_final: float32 [2, 2, 16, 16384], P(None, None, None, 'col')
- residual_final: float32 [2, 2, 16, 32768], P(None, None, None, ('row', 'col'))
All inputs are finite; a program needn't handle non-finite values.
Results may differ from a plain program's by a relative error of at most 0.009.
Values may be sent and summed in bfloat16 or wider, within the bound.
No kernel may reach another device: no remote copies, remote signals or barrier semaphores. Data moves between devices by JAX's collectives and lax.ppermute only.
A program may use at most 128 MiB of HBM per device.

v0:
```python
import math
import jax
import jax.numpy as jnp
from jax import lax
from jax.sharding import PartitionSpec as P

NV = 16
TILE = 256
RMAX = 96
F = 2
NT = 64
ITERS = 2
step_length = 0.8


def time_table(samples):
    sample_times = jnp.arange(samples, dtype=jnp.float32)[:, None]
    freq_bins = (3.0 + 5.0 * jnp.arange(F, dtype=jnp.float32))[None, :]
    phases = 2.0 * math.pi * sample_times * freq_bins / samples
    return jnp.concatenate([jnp.cos(phases), -jnp.sin(phases)], axis=1)


def apply_gate(field, gate_start, gate_stop):
    transform = time_table(NT)
    flattened = field.reshape(2 * F, -1)
    signal = jnp.dot(transform, flattened, precision=lax.Precision.HIGHEST)
    sample_index = jnp.arange(NT, dtype=jnp.int32)[:, None, None]
    window = ((sample_index >= gate_start[None]) & (sample_index < gate_stop[None])).astype(
        jnp.float32
    )
    windowed = signal * window.reshape(NT, -1)
    returned = jnp.dot(transform.T, windowed, precision=lax.Precision.HIGHEST) * (2.0 / NT)
    return returned.reshape(field.shape)


def pair_rows(field):
    real_part, imag_part = (field[0], field[1])
    upper_pair = jnp.stack([real_part, imag_part], axis=3)
    lower_pair = jnp.stack([imag_part, -real_part], axis=3)
    joined = jnp.stack([upper_pair, lower_pair], axis=1)
    return jnp.transpose(joined, (3, 0, 1, 2, 4, 5))


def combine(stacked):
    real_part = stacked[:, :, 0, :, 0] - stacked[:, :, 1, :, 1]
    imag_part = stacked[:, :, 0, :, 1] + stacked[:, :, 1, :, 0]
    joined = jnp.stack([real_part, imag_part], axis=0)
    joined = jnp.transpose(joined, (0, 2, 3, 1, 4))
    return joined.reshape(joined.shape[0], joined.shape[1], joined.shape[2], -1)


def forward(low_model, left_bases, right_bases, rank_keep):
    blocks = low_model.shape[3] // TILE
    paired = pair_rows(low_model.reshape(2, F, NV, blocks, TILE))
    coefficients = jnp.einsum(
        "jfavcs,ijfkcs->ijfavk", paired, right_bases, preferred_element_type=jnp.float32
    )
    coefficients = (coefficients * rank_keep[:, :, :, None, None, :]).astype(jnp.bfloat16)
    sendable = coefficients.reshape(coefficients.shape[0], coefficients.shape[1], F, 2, NV * RMAX)
    received = lax.all_to_all(sendable, "col", split_axis=0, concat_axis=1, tiled=True)
    received = received.reshape(received.shape[0], received.shape[1], F, 2, NV, RMAX)
    modeled = jnp.einsum(
        "ijfavk,ijfkcn->ifavcn", received, left_bases, preferred_element_type=jnp.float32
    )
    return combine(modeled)


def adjoint(residual, left_bases, right_bases, rank_keep):
    blocks = residual.shape[3] // TILE
    paired = pair_rows(residual.astype(jnp.bfloat16).reshape(2, F, NV, blocks, TILE))
    coefficients = jnp.einsum(
        "ifavcn,ijfkcn->ijfavk", paired, left_bases, preferred_element_type=jnp.float32
    )
    coefficients = coefficients.astype(jnp.bfloat16)
    sendable = coefficients.reshape(blocks, coefficients.shape[1], F, 2, NV * RMAX)
    received = lax.all_to_all(sendable, "col", split_axis=1, concat_axis=0, tiled=True)
    received = received.reshape(received.shape[0], received.shape[1], F, 2, NV, RMAX)
    received = received * rank_keep[:, :, :, None, None, :].astype(jnp.bfloat16)
    column_terms = jnp.einsum(
        "ijfavk,ijfkcs->jfavcs", received, right_bases, preferred_element_type=jnp.float32
    )
    return combine(column_terms)


def shards(model_init, observed, left_bases, right_bases, tile_ranks, gate_start, gate_stop):
    rank_index = jnp.arange(RMAX, dtype=jnp.int32)
    rank_keep = (rank_index < tile_ranks[..., None]).astype(jnp.float32)
    estimate = model_init
    low_model = model_init.astype(jnp.bfloat16)
    for iteration in range(ITERS):
        predicted = forward(low_model, left_bases, right_bases, rank_keep)
        residual = apply_gate(predicted - observed, gate_start, gate_stop)
        grad_local = adjoint(residual, left_bases, right_bases, rank_keep)
        gradient = lax.psum(grad_local.astype(jnp.bfloat16), "row").astype(jnp.float32)
        estimate = estimate - step_length * gradient
        low_model = estimate.astype(jnp.bfloat16)
    predicted = forward(low_model, left_bases, right_bases, rank_keep)
    residual = apply_gate(predicted - observed, gate_start, gate_stop)
    return (estimate, residual)


def solution(mesh):
    placed = (
        P(None, None, None, "col"),
        P(None, None, None, ("row", "col")),
        P(("row", "col"), None, None, None, None, None),
        P("row", "col", None, None, None, None),
        P("row", "col", None),
        P(None, ("row", "col")),
        P(None, ("row", "col")),
    )
    return jax.shard_map(
        shards,
        mesh=mesh,
        in_specs=placed,
        out_specs=(P(None, None, None, "col"), P(None, None, None, ("row", "col"))),
        check_vma=False,
    )
```

profile of v0, /device:TPU:6, one launch (start us, length us, event | category | flops | bytes accessed | tf_op | source)
XLA Modules:
  0.0 333.3 jit_solution(16784469923808730853)
XLA Ops:
  7.2 0.8 fusion.96
  8.0 1.0 convert_element_type.93
  9.1 9.1 %fusion.24 = bf16[16,4,2,2,16,96]{5,4,0,3,2,1:T(8,128)(2,1)S(1)} fusion(bf16[16,4,2,96,2,256,1]{5,4,3,2,1,0,6:T(2,128)(2,1)} %bitcast.384, f32[16,4,2,96]{3,0,2,1:T(8,128)S(1)} %get-tuple-element.31, bf16[2,1,16,4,2,256]{5,2,4,1,0,3:T(8,128)(2,1)S(1)} %get-tuple-element.19, bf16[2,1,16,4,2,256]{5,2,4,1,0,3:T(8,128)(2,1)S(1)} %get-tuple-element.18), kind=kOutput, calls=%fused_computation.33 | convolution fusion | flops 403963904 | bytes 13680640 | tf_op jit(solution)/shard_map/jfavcs,ijfkcs->ijfavk/dot_general | solution.py:55
  18.2 1.2 reshape.437
  19.4 1.7 copy.96
  21.1 8.4 %all-to-all-start = ((bf16[16,4,2,2,1536]{4,3,2,1,0:T(2,128)(2,1)}), bf16[16,4,2,2,1536]{4,3,2,1,0:T(2,128)(2,1)S(1)}, u32[]{:S(2)}, u32[]{:S(2)}) async-start(bf16[16,4,2,2,1536]{4,3,2,1,0:T(2,128)(2,1)} %copy.96), calls=%async_computation | async-start | bytes 1572864 | tf_op jit(solution)/shard_map/all_to_all | solution.py:60
  29.7 14.3 %all-to-all-done = bf16[16,4,2,2,1536]{4,3,2,1,0:T(2,128)(2,1)S(1)} async-done(((bf16[16,4,2,2,1536]{4,3,2,1,0:T(2,128)(2,1)}), bf16[16,4,2,2,1536]{4,3,2,1,0:T(2,128)(2,1)S(1)}, u32[]{:S(2)}, u32[]{:S(2)}) %all-to-all-start) | async-done | bytes 786464 | tf_op jit(solution)/shard_map/all_to_all | solution.py:60
  44.3 0.9 reshape.457
  45.2 6.9 %fusion.47 = f32[1,2,2,16,2,256]{5,3,4,2,1,0:T(8,128)S(1)} fusion(bf16[64,2,96,2,256,1]{4,3,2,1,0,5:T(2,128)(2,1)} %bitcast.353, bf16[64,2,2,16,96,1]{4,3,0,2,1,5:T(8,128)(2,1)S(1)} %reshape.457), kind=kOutput, calls=%fused_computation.40 | convolution fusion | flops 402653184 | bytes 13500416 | tf_op jit(solution)/shard_map/ijfavk,ijfkcn->ifavcn/dot_general | solution.py:62
  52.2 1.2 convolution_select_fusion.2
  53.4 0.6 fusion.20
  54.1 7.6 %fusion.35 = bf16[1,64,2,2,16,96]{5,4,1,3,2,0:T(8,128)(2,1)S(1)} fusion(bf16[64,2,96,2,256,1]{4,3,2,1,0,5:T(2,128)(2,1)} %bitcast.354, bf16[2,1,16,1,2,256]{5,2,4,1,0,3:T(8,128)(2,1)S(1)} %get-tuple-element.29, bf16[2,1,16,1,2,256]{5,2,4,1,0,3:T(8,128)(2,1)S(1)} %get-tuple-element.28), kind=kOutput, calls=%fused_computation.36 | convolution fusion | flops 403177472 | bytes 13434880 | tf_op jit(solution)/shard_map/ifavcn,ijfkcn->ijfavk/dot_general | solution.py:71
  61.8 1.2 reshape.442
  63.0 1.7 copy.106
  64.7 3.6 %all-to-all-start.1 = ((bf16[1,64,2,2,1536]{4,3,2,0,1:T(2,128)(2,1)}), bf16[1,64,2,2,1536]{4,3,2,0,1:T(2,128)(2,1)S(1)}, u32[]{:S(2)}, u32[]{:S(2)}) async-start(bf16[1,64,2,2,1536]{4,3,2,0,1:T(2,128)(2,1)} %copy.106), calls=%async_computation.1 | async-start | bytes 1572864 | tf_op jit(solution)/shard_map/all_to_all | solution.py:76
  68.3 0.6 all-reduce.3.cloned.1.call-start
  69.0 12.5 %all-to-all-done.1 = bf16[1,64,2,2,1536]{4,3,2,0,1:T(2,128)(2,1)S(1)} async-done(((bf16[1,64,2,2,1536]{4,3,2,0,1:T(2,128)(2,1)}), bf16[1,64,2,2,1536]{4,3,2,0,1:T(2,128)(2,1)S(1)}, u32[]{:S(2)}, u32[]{:S(2)}) %all-to-all-start.1) | async-done | bytes 786464 | tf_op jit(solution)/shard_map/all_to_all | solution.py:76
  81.6 0.9 reshape.443
  82.5 6.9 %fusion.41 = f32[4,2,2,16,2,256]{5,3,4,2,1,0:T(8,128)S(1)} fusion(bf16[16,4,2,96,2,256,1]{5,4,3,2,1,0,6:T(2,128)(2,1)} %bitcast.385, bf16[16,4,2,2,16,96]{5,4,1,0,3,2:T(8,128)(2,1)S(1)} %reshape.443, bf16[16,4,2,96]{3,1,0,2:T(4,128)(2,1)S(1)} %copy.108), kind=kOutput, calls=%fused_computation.38 | convolution fusion | flops 403046400 | bytes 13918208 | tf_op jit(solution)/shard_map/ijfavk,ijfkcs->jfavcs/dot_general | solution.py:79
  89.5 0.7 copy.210
  90.2 55.2 %all-reduce.3.cloned.1.call-done = bf16[2,2,16,1024]{3,2,1,0:T(8,128)(2,1)} async-done(((bf16[2,2,16,1024]{3,2,1,0:T(8,128)(2,1)}), bf16[2,2,16,1024]{3,2,1,0:T(8,128)(2,1)}) %all-reduce.3.cloned.1.call-update) | async-done | bytes 131088 | tf_op jit(solution)/shard_map/psum | solution.py:94
  145.4 0.9 fusion.68
  146.6 9.1 %fusion.23 = bf16[16,4,2,2,16,96]{5,4,0,3,2,1:T(8,128)(2,1)S(1)} fusion(bf16[16,4,2,96,2,256,1]{5,4,3,2,1,0,6:T(2,128)(2,1)} %bitcast.386, f32[16,4,2,96]{3,0,2,1:T(8,128)S(1)} %get-tuple-element.31, bf16[2,1,16,4,2,256]{5,2,4,1,0,3:T(8,128)(2,1)S(1)} %get-tuple-element.15, bf16[2,1,16,4,2,256]{5,2,4,1,0,3:T(8,128)(2,1)S(1)} %get-tuple-element.14), kind=kOutput, calls=%fused_computation.31 | convolution fusion | flops 403963904 | bytes 13680640 | tf_op jit(solution)/shard_map/jfavcs,ijfkcs->ijfavk/dot_general | solution.py:55
  155.7 1.2 reshape.444
  156.9 0.8 copy.119
  157.7 22.1 %all_to_all.20 = bf16[16,4,2,2,1536]{4,3,2,1,0:T(2,128)(2,1)S(1)} all-to-all(bf16[16,4,2,2,1536]{4,3,2,1,0:T(2,128)(2,1)S(1)} %copy.119), channel_id=1, replica_groups=mesh['row'=8,'col'=16] {'col'}, dimensions={0} | all-to-all | bytes 1572864 | tf_op jit(solution)/shard_map/all_to_all | solution.py:60
  180.1 0.9 reshape.469
  181.0 6.9 %fusion.50 = f32[1,2,2,16,2,256]{5,3,4,2,1,0:T(8,128)S(1)} fusion(bf16[64,2,96,2,256,1]{4,3,2,1,0,5:T(2,128)(2,1)} %bitcast.355, bf16[64,2,2,16,96,1]{4,3,0,2,1,5:T(8,128)(2,1)S(1)} %reshape.469), kind=kOutput, calls=%fused_computation.41 | convolution fusion | flops 402653184 | bytes 13500416 | tf_op jit(solution)/shard_map/ijfavk,ijfkcn->ifavcn/dot_general | solution.py:62
  188.0 1.2 convolution_select_fusion.1
  189.2 0.6 fusion.21
  189.9 7.6 %fusion.38 = bf16[1,64,2,2,16,96]{5,4,1,3,2,0:T(8,128)(2,1)S(1)} fusion(bf16[64,2,96,2,256,1]{4,3,2,1,0,5:T(2,128)(2,1)} %bitcast.356, bf16[2,1,16,1,2,256]{5,2,4,1,0,3:T(8,128)(2,1)S(1)} %get-tuple-element.27, bf16[2,1,16,1,2,256]{5,2,4,1,0,3:T(8,128)(2,1)S(1)} %get-tuple-element.26), kind=kOutput, calls=%fused_computation.37 | convolution fusion | flops 403177472 | bytes 13434880 | tf_op jit(solution)/shard_map/ifavcn,ijfkcn->ijfavk/dot_general | solution.py:71
  197.5 1.2 reshape.448
  198.7 0.8 copy.129
  199.6 17.2 %all_to_all.21 = bf16[1,64,2,2,1536]{4,3,2,0,1:T(2,128)(2,1)S(1)} all-to-all(bf16[1,64,2,2,1536]{4,3,2,0,1:T(2,128)(2,1)S(1)} %copy.129), channel_id=1, replica_groups=mesh['row'=8,'col'=16] {'col'}, dimensions={1} | all-to-all | bytes 1572864 | tf_op jit(solution)/shard_map/all_to_all | solution.py:76
  216.9 0.9 reshape.449
  217.8 6.9 %fusion.44 = f32[4,2,2,16,2,256]{5,3,4,2,1,0:T(8,128)S(1)} fusion(bf16[16,4,2,96,2,256,1]{5,4,3,2,1,0,6:T(2,128)(2,1)} %bitcast.387, bf16[16,4,2,2,16,96]{5,4,1,0,3,2:T(8,128)(2,1)S(1)} %reshape.449, bf16[16,4,2,96]{3,1,0,2:T(4,128)(2,1)S(1)} %copy.108), kind=kOutput, calls=%fused_computation.39 | convolution fusion | flops 403046400 | bytes 13918208 | tf_op jit(solution)/shard_map/ijfavk,ijfkcs->jfavcs/dot_general | solution.py:79
  224.8 0.7 copy.211
  225.5 54.9 %all-reduce.5.cloned.1.call-done = bf16[2,2,16,1024]{3,2,1,0:T(8,128)(2,1)} async-done(((bf16[2,2,16,1024]{3,2,1,0:T(8,128)(2,1)}), bf16[2,2,16,1024]{3,2,1,0:T(8,128)(2,1)}) %all-reduce.5.cloned.1.call-update) | async-done | bytes 131088 | tf_op jit(solution)/shard_map/psum | solution.py:94
  280.3 1.7 fusion.105
  282.2 9.1 %fusion.22 = bf16[16,4,2,2,16,96]{5,4,0,3,2,1:T(8,128)(2,1)S(1)} fusion(bf16[16,4,2,96,2,256,1]{5,4,3,2,1,0,6:T(2,128)(2,1)} %bitcast.388, f32[16,4,2,96]{3,0,2,1:T(8,128)S(1)} %get-tuple-element.31, bf16[2,1,16,4,2,256]{5,2,4,1,0,3:T(8,128)(2,1)S(1)} %get-tuple-element.11, bf16[2,1,16,4,2,256]{5,2,4,1,0,3:T(8,128)(2,1)S(1)} %get-tuple-element.10), kind=kOutput, calls=%fused_computation.29 | convolution fusion | flops 403963904 | bytes 13680640 | tf_op jit(solution)/shard_map/jfavcs,ijfkcs->ijfavk/dot_general | solution.py:55
  291.3 1.2 reshape.450
  292.5 0.8 copy.141
  293.3 22.2 %all_to_all.22 = bf16[16,4,2,2,1536]{4,3,2,1,0:T(2,128)(2,1)S(1)} all-to-all(bf16[16,4,2,2,1536]{4,3,2,1,0:T(2,128)(2,1)S(1)} %copy.141), channel_id=1, replica_groups=mesh['row'=8,'col'=16] {'col'}, dimensions={0} | all-to-all | bytes 1572864 | tf_op jit(solution)/shard_map/all_to_all | solution.py:60
  315.8 0.9 reshape.481
  316.7 6.9 %fusion.53 = f32[1,2,2,16,2,256]{5,3,4,2,1,0:T(8,128)S(1)} fusion(bf16[64,2,96,2,256,1]{4,3,2,1,0,5:T(2,128)(2,1)} %bitcast.357, bf16[64,2,2,16,96,1]{4,3,0,2,1,5:T(8,128)(2,1)S(1)} %reshape.481), kind=kOutput, calls=%fused_computation.42 | convolution fusion | flops 402653184 | bytes 13500416 | tf_op jit(solution)/shard_map/ijfavk,ijfkcn->ifavcn/dot_general | solution.py:62
  323.7 1.2 convolution_select_fusion
  324.9 0.6 convolution_multiply_fusion
  325.5 0.6 copy.221
  (69 shorter events, 2.3 us)
Async XLA Ops:
  7.2 22.3 %copy-start.3 = (s32[16,256]{1,0:T(8,128)S(1)}, s32[16,256]{1,0:T(8,128)}, u32[]{:S(2)}) copy-start(s32[16,256]{1,0:T(8,128)} %param.12) | copy-start | bytes 49156
  7.2 22.4 %copy-start.4 = (s32[16,256]{1,0:T(8,128)S(1)}, s32[16,256]{1,0:T(8,128)}, u32[]{:S(2)}) copy-start(s32[16,256]{1,0:T(8,128)} %param.13) | copy-start | bytes 49156
  18.2 33.9 %copy-start.1 = (f32[2,2,16,256]{3,2,1,0:T(8,128)S(1)}, f32[2,2,16,256]{3,2,1,0:T(8,128)}, u32[]{:S(2)}) copy-start(f32[2,2,16,256]{3,2,1,0:T(8,128)} %param.8) | copy-start | bytes 196612
  21.1 22.9 %all-to-all-start = ((bf16[16,4,2,2,1536]{4,3,2,1,0:T(2,128)(2,1)}), bf16[16,4,2,2,1536]{4,3,2,1,0:T(2,128)(2,1)S(1)}, u32[]{:S(2)}, u32[]{:S(2)}) async-start(bf16[16,4,2,2,1536]{4,3,2,1,0:T(2,128)(2,1)} %copy.96), calls=%async_computation | async-start | bytes 1572864 | tf_op jit(solution)/shard_map/all_to_all | solution.py:60
  61.8 83.7 %copy-start = (f32[2,2,16,1024]{3,2,1,0:T(8,128)S(1)}, f32[2,2,16,1024]{3,2,1,0:T(8,128)}, u32[]{:S(2)}) copy-start(f32[2,2,16,1024]{3,2,1,0:T(8,128)} %param.7) | copy-start | bytes 786436
  64.7 16.8 %all-to-all-start.1 = ((bf16[1,64,2,2,1536]{4,3,2,0,1:T(2,128)(2,1)}), bf16[1,64,2,2,1536]{4,3,2,0,1:T(2,128)(2,1)S(1)}, u32[]{:S(2)}, u32[]{:S(2)}) async-start(bf16[1,64,2,2,1536]{4,3,2,0,1:T(2,128)(2,1)} %copy.106), calls=%async_computation.1 | async-start | bytes 1572864 | tf_op jit(solution)/shard_map/all_to_all | solution.py:76
  68.3 77.1 %all-reduce.3.cloned.1.call-start = ((), (), s32[]{:S(2)}) async-start(), calls=%async_computation.5 | async-start | bytes 262144 | tf_op jit(solution)/shard_map/psum | solution.py:94
  90.2 190.2 %all-reduce.5.cloned.1.call-start = ((), (), s32[]{:S(2)}) async-start(), calls=%async_computation.6 | async-start | bytes 262144 | tf_op jit(solution)/shard_map/psum | solution.py:94
  197.5 82.8 %copy-start.2 = (bf16[2,2,16,1024]{3,2,1,0:T(8,128)(2,1)S(1)}, bf16[2,2,16,1024]{3,2,1,0:T(8,128)(2,1)}, u32[]{:S(2)}) copy-start(bf16[2,2,16,1024]{3,2,1,0:T(8,128)(2,1)} %all-reduce.3.cloned.1.call-done) | copy-start | bytes 393220
Sparse Core Ops, SparseCore 0:
  90.3 55.1 all-reduce.2
  225.6 54.6 all-reduce.4
where the time goes:
time: 338 us; the launch traced here: 333 us
  waiting for transfers between devices  137 us (41%)
  matrix products  82.3 us (24%)
  blocking collectives  61.5 us (18%)
  local copies, waits for them, and re-layouts  20.1 us (6%)
  between operations  14.9 us (4%)
  starting transfers between devices  12.7 us (4%)
  other arithmetic  4.85 us (1%)
    psum x2, waiting for transfers between devices, shards(): lax.psum(grad_local.astype(jnp.bfloat16), 'row').astype(jnp.float32)  110 us
    all_to_all x2, blocking collectives, forward(): lax.all_to_all(sendable, 'col', split_axis=0, concat_axis=1, tiled=True)  44.3 us
    dot_general x3, matrix products, forward(): jnp.einsum('jfavcs,ijfkcs->ijfavk', paired, right_bases, preferred_elemen...  27.3 us
    dot_general x3, matrix products, forward(): jnp.einsum('ijfavk,ijfkcn->ifavcn', received, left_bases, preferred_eleme...  20.6 us
    all_to_all x1, blocking collectives, adjoint(): lax.all_to_all(sendable, 'col', split_axis=1, concat_axis=0, tiled=True)  17.2 us
    dot_general x2, matrix products, adjoint(): jnp.einsum('ifavcn,ijfkcn->ijfavk', paired, left_bases, preferred_element...  15.2 us
    all_to_all x1, waiting for transfers between devices, forward(): lax.all_to_all(sendable, 'col', split_axis=0, concat_axis=1, tiled=True)  14.3 us
    dot_general x2, matrix products, adjoint(): jnp.einsum('ijfavk,ijfkcs->jfavcs', received, right_bases, preferred_elem...  13.8 us
  transfers between devices with their start and end apart: 4, of which 4 were waited for; matrix products, arithmetic and copies ran while one was open for 0% of the time, Pallas kernels for 0%

commit v1 on v0

--- a/solution.py
+++ b/solution.py
@@ -57,7 +57,10 @@
     )
     coefficients = (coefficients * rank_keep[:, :, :, None, None, :]).astype(jnp.bfloat16)
     sendable = coefficients.reshape(coefficients.shape[0], coefficients.shape[1], F, 2, NV * RMAX)
-    received = lax.all_to_all(sendable, "col", split_axis=0, concat_axis=1, tiled=True)
+    received = jnp.concatenate(
+        lax.all_to_all(jnp.stack(jnp.split(sendable, lax.axis_size("col"), axis=0)), "col", 0, 0),
+        axis=1,
+    )
     received = received.reshape(received.shape[0], received.shape[1], F, 2, NV, RMAX)
     modeled = jnp.einsum(
         "ijfavk,ijfkcn->ifavcn", received, left_bases, preferred_element_type=jnp.float32

time: 338 us -> 352 us (1.041)
  local copies, waits for them, and re-layouts: 20.1 us -> 32.5 us
    unnamed x18 -> x63, local copies, waits for them, and re-layouts: 0.84 us -> 11.9 us
    another operation x3 -> x54, local copies, waits for them, and re-layouts: 2.77 us -> 10.2 us  [the longest x51 7.44 us: forward(): jnp.stack(jnp.split(sendable, lax.axis_size('col'), axis=0))]
    reshape x6 -> x0, local copies, waits for them, and re-layouts: 6.95 us -> none  [forward(): coefficients.reshape(coefficients.shape[0], coefficients.shape[1], F, 2,...]
where the time goes in v1:
time: 352 us; the launch traced here: 347 us
  waiting for transfers between devices  137 us (39%)
  matrix products  82.3 us (23%)
  blocking collectives  61.6 us (18%)
  local copies, waits for them, and re-layouts  32.5 us (9%)
  between operations  15.4 us (4%)
  starting transfers between devices  12.4 us (4%)
  other arithmetic  4.85 us (1%)
    psum x2, waiting for transfers between devices, shards(): lax.psum(grad_local.astype(jnp.bfloat16), 'row').astype(jnp.float32)  110 us
    all_to_all x2, blocking collectives, forward(): lax.all_to_all(jnp.stack(jnp.split(sendable, lax.axis_size('col'), axis=0...  44.3 us
    dot_general x3, matrix products, forward(): jnp.einsum('jfavcs,ijfkcs->ijfavk', paired, right_bases, preferred_elemen...  27.3 us
    dot_general x3, matrix products, forward(): jnp.einsum('ijfavk,ijfkcn->ifavcn', received, left_bases, preferred_eleme...  20.6 us
    all_to_all x1, blocking collectives, adjoint(): lax.all_to_all(sendable, 'col', split_axis=1, concat_axis=0, tiled=True)  17.3 us
    dot_general x2, matrix products, adjoint(): jnp.einsum('ifavcn,ijfkcn->ijfavk', paired, left_bases, preferred_element...  15.2 us
    all_to_all x1, waiting for transfers between devices, forward(): lax.all_to_all(jnp.stack(jnp.split(sendable, lax.axis_size('col'), axis=0...  14.3 us
    dot_general x2, matrix products, adjoint(): jnp.einsum('ijfavk,ijfkcs->jfavcs', received, right_bases, preferred_elem...  13.8 us
  transfers between devices with their start and end apart: 4, of which 4 were waited for; matrix products, arithmetic and copies ran while one was open for 0% of the time, Pallas kernels for 0%

profile of v1, /device:TPU:6, one launch (start us, length us, event | category | flops | bytes accessed | tf_op | source)
XLA Modules:
  0.0 346.6 jit_solution(14716226067238571003)
XLA Ops:
  7.2 0.8 fusion.96
  8.0 1.0 convert_element_type.93
  9.1 9.1 %fusion.24 = bf16[16,4,2,2,16,96]{5,4,0,3,2,1:T(8,128)(2,1)S(1)} fusion(bf16[16,4,2,96,2,256,1]{5,4,3,2,1,0,6:T(2,128)(2,1)} %bitcast.564, f32[16,4,2,96]{3,0,2,1:T(8,128)S(1)} %get-tuple-element.79, bf16[2,1,16,4,2,256]{5,2,4,1,0,3:T(8,128)(2,1)S(1)} %get-tuple-element.67, bf16[2,1,16,4,2,256]{5,2,4,1,0,3:T(8,128)(2,1)S(1)} %get-tuple-element.66), kind=kOutput, calls=%fused_computation.33 | convolution fusion | flops 403963904 | bytes 13680640 | tf_op jit(solution)/shard_map/jfavcs,ijfkcs->ijfavk/dot_general | solution.py:55
  21.4 0.7 constant_dynamic-update-slice_fusion.14
  22.1 0.7 constant_dynamic-update-slice_fusion.13
  23.4 0.6 constant_dynamic-update-slice_fusion.11
  24.7 0.7 constant_dynamic-update-slice_fusion.9
  25.3 0.6 constant_dynamic-update-slice_fusion.8
  26.0 0.7 constant_dynamic-update-slice_fusion.7
  26.7 0.7 constant_dynamic-update-slice_fusion.6
  27.3 0.7 constant_dynamic-update-slice_fusion.5
  28.6 0.7 constant_dynamic-update-slice_fusion.3
  29.9 0.7 constant_dynamic-update-slice_fusion.1
  30.6 0.7 constant_dynamic-update-slice_fusion
  31.2 8.6 %all-to-all-start = ((bf16[16,1,4,2,2,1536]{5,4,3,2,1,0:T(2,128)(2,1)}), bf16[16,1,4,2,2,1536]{5,4,3,2,1,0:T(2,128)(2,1)S(1)}, u32[]{:S(2)}, u32[]{:S(2)}) async-start(bf16[16,1,4,2,2,1536]{5,4,3,2,1,0:T(2,128)(2,1)} %constant_dynamic-update-slice_fusion), calls=%async_computation | async-start | bytes 1572864 | tf_op jit(solution)/shard_map/all_to_all | solution.py:61
  40.0 14.3 %all-to-all-done = bf16[16,1,4,2,2,1536]{5,4,3,2,1,0:T(2,128)(2,1)S(1)} async-done(((bf16[16,1,4,2,2,1536]{5,4,3,2,1,0:T(2,128)(2,1)}), bf16[16,1,4,2,2,1536]{5,4,3,2,1,0:T(2,128)(2,1)S(1)}, u32[]{:S(2)}, u32[]{:S(2)}) %all-to-all-start) | async-done | bytes 786464 | tf_op jit(solution)/shard_map/all_to_all | solution.py:61
  54.6 0.9 reshape.529
  55.5 6.9 %fusion.47 = f32[1,2,2,16,2,256]{5,3,4,2,1,0:T(8,128)S(1)} fusion(bf16[64,2,96,2,256,1]{4,3,2,1,0,5:T(2,128)(2,1)} %bitcast.533, bf16[64,2,2,16,96,1]{4,3,0,2,1,5:T(8,128)(2,1)S(1)} %reshape.529), kind=kOutput, calls=%fused_computation.40 | convolution fusion | flops 402653184 | bytes 13500416 | tf_op jit(solution)/shard_map/ijfavk,ijfkcn->ifavcn/dot_general | solution.py:65
  62.5 1.2 convolution_select_fusion.2
  64.4 7.6 %fusion.35 = bf16[1,64,2,2,16,96]{5,4,1,3,2,0:T(8,128)(2,1)S(1)} fusion(bf16[64,2,96,2,256,1]{4,3,2,1,0,5:T(2,128)(2,1)} %bitcast.534, bf16[2,1,16,1,2,256]{5,2,4,1,0,3:T(8,128)(2,1)S(1)} %get-tuple-element.77, bf16[2,1,16,1,2,256]{5,2,4,1,0,3:T(8,128)(2,1)S(1)} %get-tuple-element.76), kind=kOutput, calls=%fused_computation.36 | convolution fusion | flops 403177472 | bytes 13434880 | tf_op jit(solution)/shard_map/ifavcn,ijfkcn->ijfavk/dot_general | solution.py:74
  72.1 1.2 reshape.516
  73.3 1.7 copy.105
  75.0 3.6 %all-to-all-start.1 = ((bf16[1,64,2,2,1536]{4,3,2,0,1:T(2,128)(2,1)}), bf16[1,64,2,2,1536]{4,3,2,0,1:T(2,128)(2,1)S(1)}, u32[]{:S(2)}, u32[]{:S(2)}) async-start(bf16[1,64,2,2,1536]{4,3,2,0,1:T(2,128)(2,1)} %copy.105), calls=%async_computation.1 | async-start | bytes 1572864 | tf_op jit(solution)/shard_map/all_to_all | solution.py:79
  78.8 12.9 %all-to-all-done.1 = bf16[1,64,2,2,1536]{4,3,2,0,1:T(2,128)(2,1)S(1)} async-done(((bf16[1,64,2,2,1536]{4,3,2,0,1:T(2,128)(2,1)}), bf16[1,64,2,2,1536]{4,3,2,0,1:T(2,128)(2,1)S(1)}, u32[]{:S(2)}, u32[]{:S(2)}) %all-to-all-start.1) | async-done | bytes 786464 | tf_op jit(solution)/shard_map/all_to_all | solution.py:79
  91.9 0.9 reshape.517
  92.8 6.9 %fusion.41 = f32[4,2,2,16,2,256]{5,3,4,2,1,0:T(8,128)S(1)} fusion(bf16[16,4,2,96,2,256,1]{5,4,3,2,1,0,6:T(2,128)(2,1)} %bitcast.565, bf16[16,4,2,2,16,96]{5,4,1,0,3,2:T(8,128)(2,1)S(1)} %reshape.517, bf16[16,4,2,96]{3,1,0,2:T(4,128)(2,1)S(1)} %copy.107), kind=kOutput, calls=%fused_computation.38 | convolution fusion | flops 403046400 | bytes 13918208 | tf_op jit(solution)/shard_map/ijfavk,ijfkcs->jfavcs/dot_general | solution.py:82
  99.8 0.7 copy.207
  100.5 55.2 %all-reduce.3.cloned.1.call-done = bf16[2,2,16,1024]{3,2,1,0:T(8,128)(2,1)} async-done(((bf16[2,2,16,1024]{3,2,1,0:T(8,128)(2,1)}), bf16[2,2,16,1024]{3,2,1,0:T(8,128)(2,1)}) %all-reduce.3.cloned.1.call-update) | async-done | bytes 131088 | tf_op jit(solution)/shard_map/psum | solution.py:97
  155.7 0.9 fusion.68
  156.8 9.1 %fusion.23 = bf16[16,4,2,2,16,96]{5,4,0,3,2,1:T(8,128)(2,1)S(1)} fusion(bf16[16,4,2,96,2,256,1]{5,4,3,2,1,0,6:T(2,128)(2,1)} %bitcast.566, f32[16,4,2,96]{3,0,2,1:T(8,128)S(1)} %get-tuple-element.79, bf16[2,1,16,4,2,256]{5,2,4,1,0,3:T(8,128)(2,1)S(1)} %get-tuple-element.63, bf16[2,1,16,4,2,256]{5,2,4,1,0,3:T(8,128)(2,1)S(1)} %get-tuple-element.62), kind=kOutput, calls=%fused_computation.31 | convolution fusion | flops 403963904 | bytes 13680640 | tf_op jit(solution)/shard_map/jfavcs,ijfkcs->ijfavk/dot_general | solution.py:55
  169.3 22.1 %all_to_all.33 = bf16[16,1,4,2,2,1536]{5,4,3,2,1,0:T(2,128)(2,1)S(1)} all-to-all(bf16[16,1,4,2,2,1536]{5,4,3,2,1,0:T(2,128)(2,1)S(1)} %constant_dynamic-update-slice_fusion.16), channel_id=1, replica_groups=mesh['row'=8,'col'=16] {'col'}, dimensions={0} | all-to-all | bytes 1572864 | tf_op jit(solution)/shard_map/all_to_all | solution.py:61
  191.7 0.9 reshape.541
  192.6 6.9 %fusion.50 = f32[1,2,2,16,2,256]{5,3,4,2,1,0:T(8,128)S(1)} fusion(bf16[64,2,96,2,256,1]{4,3,2,1,0,5:T(2,128)(2,1)} %bitcast.535, bf16[64,2,2,16,96,1]{4,3,0,2,1,5:T(8,128)(2,1)S(1)} %reshape.541), kind=kOutput, calls=%fused_computation.41 | convolution fusion | flops 402653184 | bytes 13500416 | tf_op jit(solution)/shard_map/ijfavk,ijfkcn->ifavcn/dot_general | solution.py:65
  199.6 1.2 convolution_select_fusion.1
  201.5 7.6 %fusion.38 = bf16[1,64,2,2,16,96]{5,4,1,3,2,0:T(8,128)(2,1)S(1)} fusion(bf16[64,2,96,2,256,1]{4,3,2,1,0,5:T(2,128)(2,1)} %bitcast.536, bf16[2,1,16,1,2,256]{5,2,4,1,0,3:T(8,128)(2,1)S(1)} %get-tuple-element.75, bf16[2,1,16,1,2,256]{5,2,4,1,0,3:T(8,128)(2,1)S(1)} %get-tuple-element.74), kind=kOutput, calls=%fused_computation.37 | convolution fusion | flops 403177472 | bytes 13434880 | tf_op jit(solution)/shard_map/ifavcn,ijfkcn->ijfavk/dot_general | solution.py:74
  209.2 1.2 reshape.521
  210.4 0.8 copy.127
  211.2 17.3 %all_to_all.34 = bf16[1,64,2,2,1536]{4,3,2,0,1:T(2,128)(2,1)S(1)} all-to-all(bf16[1,64,2,2,1536]{4,3,2,0,1:T(2,128)(2,1)S(1)} %copy.127), channel_id=1, replica_groups=mesh['row'=8,'col'=16] {'col'}, dimensions={1} | all-to-all | bytes 1572864 | tf_op jit(solution)/shard_map/all_to_all | solution.py:79
  228.6 0.9 reshape.522
  229.5 6.9 %fusion.44 = f32[4,2,2,16,2,256]{5,3,4,2,1,0:T(8,128)S(1)} fusion(bf16[16,4,2,96,2,256,1]{5,4,3,2,1,0,6:T(2,128)(2,1)} %bitcast.567, bf16[16,4,2,2,16,96]{5,4,1,0,3,2:T(8,128)(2,1)S(1)} %reshape.522, bf16[16,4,2,96]{3,1,0,2:T(4,128)(2,1)S(1)} %copy.107), kind=kOutput, calls=%fused_computation.39 | convolution fusion | flops 403046400 | bytes 13918208 | tf_op jit(solution)/shard_map/ijfavk,ijfkcs->jfavcs/dot_general | solution.py:82
  236.4 0.7 copy.208
  237.1 54.9 %all-reduce.5.cloned.1.call-done = bf16[2,2,16,1024]{3,2,1,0:T(8,128)(2,1)} async-done(((bf16[2,2,16,1024]{3,2,1,0:T(8,128)(2,1)}), bf16[2,2,16,1024]{3,2,1,0:T(8,128)(2,1)}) %all-reduce.5.cloned.1.call-update) | async-done | bytes 131088 | tf_op jit(solution)/shard_map/psum | solution.py:97
  292.0 1.7 fusion.105
  293.8 9.1 %fusion.22 = bf16[16,4,2,2,16,96]{5,4,0,3,2,1:T(8,128)(2,1)S(1)} fusion(bf16[16,4,2,96,2,256,1]{5,4,3,2,1,0,6:T(2,128)(2,1)} %bitcast.568, f32[16,4,2,96]{3,0,2,1:T(8,128)S(1)} %get-tuple-element.79, bf16[2,1,16,4,2,256]{5,2,4,1,0,3:T(8,128)(2,1)S(1)} %get-tuple-element.59, bf16[2,1,16,4,2,256]{5,2,4,1,0,3:T(8,128)(2,1)S(1)} %get-tuple-element.58), kind=kOutput, calls=%fused_computation.29 | convolution fusion | flops 403963904 | bytes 13680640 | tf_op jit(solution)/shard_map/jfavcs,ijfkcs->ijfavk/dot_general | solution.py:55
  306.3 22.2 %all_to_all.35 = bf16[16,1,4,2,2,1536]{5,4,3,2,1,0:T(2,128)(2,1)S(1)} all-to-all(bf16[16,1,4,2,2,1536]{5,4,3,2,1,0:T(2,128)(2,1)S(1)} %constant_dynamic-update-slice_fusion.32), channel_id=1, replica_groups=mesh['row'=8,'col'=16] {'col'}, dimensions={0} | all-to-all | bytes 1572864 | tf_op jit(solution)/shard_map/all_to_all | solution.py:61
  328.8 0.9 reshape.553
  329.8 6.9 %fusion.53 = f32[1,2,2,16,2,256]{5,3,4,2,1,0:T(8,128)S(1)} fusion(bf16[64,2,96,2,256,1]{4,3,2,1,0,5:T(2,128)(2,1)} %bitcast.537, bf16[64,2,2,16,96,1]{4,3,0,2,1,5:T(8,128)(2,1)S(1)} %reshape.553), kind=kOutput, calls=%fused_computation.42 | convolution fusion | flops 402653184 | bytes 13500416 | tf_op jit(solution)/shard_map/ijfavk,ijfkcn->ifavcn/dot_general | solution.py:65
  336.7 1.2 convolution_select_fusion
  (162 shorter events, 17.2 us)
Async XLA Ops:
  7.2 32.6 %copy-start.3 = (s32[16,256]{1,0:T(8,128)S(1)}, s32[16,256]{1,0:T(8,128)}, u32[]{:S(2)}) copy-start(s32[16,256]{1,0:T(8,128)} %param.12) | copy-start | bytes 49156
  7.2 32.7 %copy-start.4 = (s32[16,256]{1,0:T(8,128)S(1)}, s32[16,256]{1,0:T(8,128)}, u32[]{:S(2)}) copy-start(s32[16,256]{1,0:T(8,128)} %param.13) | copy-start | bytes 49156
  18.2 44.2 %copy-start.1 = (f32[2,2,16,256]{3,2,1,0:T(8,128)S(1)}, f32[2,2,16,256]{3,2,1,0:T(8,128)}, u32[]{:S(2)}) copy-start(f32[2,2,16,256]{3,2,1,0:T(8,128)} %param.8) | copy-start | bytes 196612
  31.2 23.1 %all-to-all-start = ((bf16[16,1,4,2,2,1536]{5,4,3,2,1,0:T(2,128)(2,1)}), bf16[16,1,4,2,2,1536]{5,4,3,2,1,0:T(2,128)(2,1)S(1)}, u32[]{:S(2)}, u32[]{:S(2)}) async-start(bf16[16,1,4,2,2,1536]{5,4,3,2,1,0:T(2,128)(2,1)} %constant_dynamic-update-slice_fusion), calls=%async_computation | async-start | bytes 1572864 | tf_op jit(solution)/shard_map/all_to_all | solution.py:61
  72.0 83.7 %copy-start = (f32[2,2,16,1024]{3,2,1,0:T(8,128)S(1)}, f32[2,2,16,1024]{3,2,1,0:T(8,128)}, u32[]{:S(2)}) copy-start(f32[2,2,16,1024]{3,2,1,0:T(8,128)} %param.7) | copy-start | bytes 786436
  75.0 16.8 %all-to-all-start.1 = ((bf16[1,64,2,2,1536]{4,3,2,0,1:T(2,128)(2,1)}), bf16[1,64,2,2,1536]{4,3,2,0,1:T(2,128)(2,1)S(1)}, u32[]{:S(2)}, u32[]{:S(2)}) async-start(bf16[1,64,2,2,1536]{4,3,2,0,1:T(2,128)(2,1)} %copy.105), calls=%async_computation.1 | async-start | bytes 1572864 | tf_op jit(solution)/shard_map/all_to_all | solution.py:79
  78.6 77.1 %all-reduce.3.cloned.1.call-start = ((), (), s32[]{:S(2)}) async-start(), calls=%async_computation.5 | async-start | bytes 262144 | tf_op jit(solution)/shard_map/psum | solution.py:97
  100.4 191.6 %all-reduce.5.cloned.1.call-start = ((), (), s32[]{:S(2)}) async-start(), calls=%async_computation.6 | async-start | bytes 262144 | tf_op jit(solution)/shard_map/psum | solution.py:97
  209.2 82.9 %copy-start.2 = (bf16[2,2,16,1024]{3,2,1,0:T(8,128)(2,1)S(1)}, bf16[2,2,16,1024]{3,2,1,0:T(8,128)(2,1)}, u32[]{:S(2)}) copy-start(bf16[2,2,16,1024]{3,2,1,0:T(8,128)(2,1)} %all-reduce.3.cloned.1.call-done) | copy-start | bytes 393220
Sparse Core Ops, SparseCore 0:
  100.6 55.0 all-reduce.2
  237.3 54.6 all-reduce.4
